TPU v7x, 32 devices: a whole 2x2x4 slice. The times are simulated.
32 devices in a mesh: queue: 16 (over z, y, x), tp: 2 (over core).
Axes of the slice: x: 2, y: 2, z: 4, core: 2. Of those that a mesh axis runs over, the one named last changes fastest.
Arguments:
- latent: bfloat16 [16, 128, 3072], P('queue', None, 'tp'), may hold values from -6 to 6
- step_index: int32 [16], P('queue'), may hold values from 0 to 49
- back_reach: int32 [16], P('queue'), may hold values from 1 to 2
- ahead_reach: int32 [16], P('queue'), may hold values from 1 to 2
- level_mod: float32 [50, 2, 3072], replicated, may hold values from -20 to 20
- text_mod: float32 [2, 2, 3072], replicated, may hold values from -3 to 3
- w_qkv: bfloat16 [3, 3072, 1536], P(None, None, 'tp'), may hold values from -0.109375 to 0.109375
- w_out: bfloat16 [1536, 3072], P('tp'), may hold values from -0.15625 to 0.15625
- keep_coef: float32 [50], replicated, may hold values from 0.6 to 1
- noise_coef: float32 [50], replicated, may hold values from 0.2 to 1
Outputs:
- rolled: bfloat16 [16, 128, 3072], P('queue', None, 'tp')
All inputs are finite; a program needn't handle non-finite values.
Results may differ from a plain program's by a relative error of at most 0.012.
The roundings to bfloat16 on the way count: a program that leaves them out, or rounds other values in their place, can miss the bound.
Values may be sent and summed in bfloat16 or wider, within the bound.
A program may use at most 128 MiB of HBM per device.

v0:
```python
import jax
import jax.numpy as jnp
from jax import lax
from jax.sharding import PartitionSpec as P

HDIM = 64
REACH = 2


epsilon = 1e-06
guidance = 6.0


def passed_along(value, axis, steps):
    count = lax.axis_size(axis)
    initial, last = (max(0, -steps), min(count, count - steps))
    return lax.ppermute(value, axis, [(source, source + steps) for source in range(initial, last)])


def shifted(value, axis, steps):
    count = lax.axis_size(axis)
    pairs = [(source, (source + steps) % count) for source in range(count)]
    return lax.ppermute(value, axis, pairs)


def attend(query_rows, key_block, value_block, key_mask, local_heads):
    tokens = query_rows.shape[0]
    query_heads = query_rows.reshape(tokens, local_heads, HDIM)
    key_heads = key_block.reshape(key_block.shape[0], local_heads, HDIM)
    value_heads = value_block.reshape(value_block.shape[0], local_heads, HDIM)
    scores = jnp.einsum(
        "shd,khd->hsk", query_heads, key_heads, preferred_element_type=jnp.float32
    ) * HDIM ** (-0.5)
    scores = jnp.where(key_mask[None, None, :], scores, -1e30)
    top = jnp.max(scores, axis=-1, keepdims=True)
    expon = jnp.exp(scores - top)
    probs = (expon / jnp.sum(expon, axis=-1, keepdims=True)).astype(jnp.bfloat16)
    attended = jnp.einsum("hsk,khd->shd", probs, value_heads, preferred_element_type=jnp.float32)
    return attended.astype(jnp.bfloat16).reshape(tokens, local_heads * HDIM)


def on_device(
    latent,
    step_index,
    back_reach,
    ahead_reach,
    level_mod,
    text_mod,
    w_qkv,
    w_out,
    keep_coef,
    noise_coef,
):
    gathered = lax.all_gather(latent, "tp", axis=2, tiled=True)[0].astype(jnp.float32)
    tokens = gathered.shape[0]
    row_mean = jnp.mean(gathered, axis=-1, keepdims=True)
    centred = gathered - row_mean
    spread = jnp.mean(centred * centred, axis=-1, keepdims=True)
    unit_rows = centred * lax.rsqrt(spread + epsilon)
    levels = level_mod.shape[0]
    picker = (jnp.arange(levels, dtype=jnp.int32) == step_index[0]).astype(jnp.float32)
    modulation = jnp.einsum("l,lcd->cd", picker, level_mod, precision=lax.Precision.HIGHEST)
    shift_terms = modulation[0][None, :] + text_mod[:, 0]
    scale_terms = modulation[1][None, :] + text_mod[:, 1]
    normed = (unit_rows[None] * (1.0 + scale_terms[:, None, :]) + shift_terms[:, None, :]).astype(
        jnp.bfloat16
    )
    normed = normed.reshape(2 * tokens, normed.shape[2])
    queries = jnp.dot(normed, w_qkv[0], preferred_element_type=jnp.float32).astype(jnp.bfloat16)
    key_value = jnp.einsum(
        "rd,cde->cre", normed, w_qkv[1:], preferred_element_type=jnp.float32
    ).astype(jnp.bfloat16)
    local_heads = queries.shape[1] // HDIM
    behind = []
    ahead = []
    for distance in range(REACH):
        behind.append(passed_along(key_value, "queue", distance + 1))
        ahead.append(passed_along(key_value, "queue", -(distance + 1)))
    blocks = behind[::-1] + [key_value] + ahead
    stacked = jnp.stack(blocks)
    position = lax.axis_index("queue")
    queue_len = lax.axis_size("queue")
    offsets = jnp.arange(-REACH, REACH + 1, dtype=jnp.int32)
    target = position + offsets
    allowed = (
        (offsets >= -back_reach[0])
        & (offsets <= ahead_reach[0])
        & (target >= 0)
        & (target < queue_len)
    )
    key_mask = jnp.repeat(allowed, tokens)
    span = 2 * REACH + 1
    outputs = []
    for branch in range(2):
        rows_from = branch * tokens
        key_block = stacked[:, 0, rows_from : rows_from + tokens].reshape(
            span * tokens, stacked.shape[3]
        )
        value_block = stacked[:, 1, rows_from : rows_from + tokens].reshape(
            span * tokens, stacked.shape[3]
        )
        outputs.append(
            attend(
                queries[rows_from : rows_from + tokens],
                key_block,
                value_block,
                key_mask,
                local_heads,
            )
        )
    cond_rows = outputs[0].astype(jnp.float32)
    plain_rows = outputs[1].astype(jnp.float32)
    mixture = plain_rows + guidance * (cond_rows - plain_rows)
    upper_part = mixture.astype(jnp.bfloat16)
    lower_part = (mixture - upper_part.astype(jnp.float32)).astype(jnp.bfloat16)
    partial_value = jnp.dot(upper_part, w_out, preferred_element_type=jnp.float32) + jnp.dot(
        lower_part, w_out, preferred_element_type=jnp.float32
    )
    guided = lax.psum_scatter(partial_value, "tp", scatter_dimension=1, tiled=True)
    keep_now = jnp.sum(picker * keep_coef)
    noise_now = jnp.sum(picker * noise_coef)
    renewed = (keep_now * latent[0].astype(jnp.float32) - noise_now * guided).astype(jnp.bfloat16)[
        None
    ]
    return shifted(renewed, "queue", 1)


def solution(mesh):
    return jax.shard_map(
        on_device,
        mesh=mesh,
        in_specs=(
            P("queue", None, "tp"),
            P("queue"),
            P("queue"),
            P("queue"),
            P(),
            P(),
            P(None, None, "tp"),
            P("tp", None),
            P(),
            P(),
        ),
        out_specs=P("queue", None, "tp"),
        check_vma=False,
    )
```

profile of v0, /device:TPU:0, one launch (start us, length us, event | category | flops | bytes accessed | tf_op | source)
XLA Modules:
  0.0 148.8 jit_solution(17677777736252471975)
XLA Ops:
  8.7 2.7 %all_gather.3 = bf16[1,128,3072]{2,1,0:T(8,128)(2,1)S(1)} all-gather(bf16[1,128,1536]{2,1,0:T(8,128)(2,1)} %param.10), channel_id=1, replica_groups=mesh['queue'=16,'tp'=2] {'tp'}, dimensions={2}, use_global_device_ids=true | all-gather | bytes 1179648 | tf_op jit(solution)/shard_map/all_gather | solution.py:54
  12.8 6.3 %fusion.22 = bf16[256,2,768]{2,0,1:T(8,128)(2,1)S(1)} fusion(bf16[256,3072,1]{1,0,2:T(8,128)(2,1)S(1)} %bitcast.96, bf16[3,3072,768]{2,1,0:T(8,128)(2,1)} %param.16), kind=kOutput, calls=%fused_computation.33 | convolution fusion | flops 2416312320 | bytes 11796480 | tf_op jit(solution)/shard_map/rd,cde->cre/dot_general | solution.py:70
  19.1 5.7 %collective-permute-start = (bf16[2,256,768]{2,1,0:T(8,128)(2,1)S(1)}, bf16[2,256,768]{2,1,0:T(8,128)(2,1)}, u32[]{:S(2)}, u32[]{:S(2)}) collective-permute-start(bf16[2,256,768]{2,1,0:T(8,128)(2,1)S(1)} %bitcast.98), channel_id=1, source_target_pairs={{0,4},{2,6},{4,8},{6,10},{8,12},{10,14},{12,16},{14,18},{16,20},{1... | collective-permute-start | bytes 2359304 | tf_op jit(solution)/shard_map/ppermute | solution.py:17
  24.8 4.3 %collective-permute-start.1 = (bf16[2,256,768]{2,1,0:T(8,128)(2,1)S(1)}, bf16[2,256,768]{2,1,0:T(8,128)(2,1)}, u32[]{:S(2)}, u32[]{:S(2)}) collective-permute-start(bf16[2,256,768]{2,1,0:T(8,128)(2,1)S(1)} %bitcast.99), channel_id=1, source_target_pairs={{0,2},{2,4},{4,6},{6,8},{8,10},{10,12},{12,14},{14,16},{16,18},{18... | collective-permute-start | bytes 2359304 | tf_op jit(solution)/shard_map/ppermute | solution.py:17
  31.7 3.8 %fusion.27 = bf16[256,768]{1,0:T(8,128)(2,1)S(1)} fusion(bf16[256,3072]{1,0:T(8,128)(2,1)S(1)} %bitcast.97, bf16[3,3072,768]{2,1,0:T(8,128)(2,1)} %param.16), kind=kOutput, calls=%fused_computation.36 | convolution fusion | flops 1208156160 | bytes 6684672 | tf_op jit(solution)/shard_map/dot_general | solution.py:69
  37.8 20.0 %collective-permute-done = bf16[2,256,768]{2,1,0:T(8,128)(2,1)} collective-permute-done((bf16[2,256,768]{2,1,0:T(8,128)(2,1)S(1)}, bf16[2,256,768]{2,1,0:T(8,128)(2,1)}, u32[]{:S(2)}, u32[]{:S(2)}) %collective-permute-start) | collective-permute-done | bytes 786464 | tf_op jit(solution)/shard_map/ppermute | solution.py:17
  59.0 2.8 %collective-permute-done.1 = bf16[2,256,768]{2,1,0:T(8,128)(2,1)} collective-permute-done((bf16[2,256,768]{2,1,0:T(8,128)(2,1)S(1)}, bf16[2,256,768]{2,1,0:T(8,128)(2,1)}, u32[]{:S(2)}, u32[]{:S(2)}) %collective-permute-start.1) | collective-permute-done | bytes 786464 | tf_op jit(solution)/shard_map/ppermute | solution.py:17
  64.4 2.0 %fusion.51 = (bf16[5,1,128,768]{3,2,1,0:T(8,128)(2,1)}, bf16[5,1,128,768]{3,2,1,0:T(8,128)(2,1)}, bf16[5,1,128,768]{3,2,1,0:T(8,128)(2,1)}, bf16[5,1,128,768]{3,2,1,0:T(8,128)(2,1)}) fusion(bf16[5,2,256,768]{3,2,1,0:T(8,128)(2,1)S(1)} %bitcast_dynamic-update-slice_fusion.1), kind=kLoop, calls=%fused_computation.76 | loop fusion | bytes 7864320 | tf_op jit(solution)/shard_map/slice | solution.py:96
  66.3 2.0 %copy.19 = bf16[5,1,128,768]{2,0,3,1:T(8,128)(2,1)S(1)} copy(bf16[5,1,128,768]{3,2,1,0:T(8,128)(2,1)} %get-tuple-element.5) | data formatting | bytes 1966080 | tf_op jit(solution)/shard_map/slice | solution.py:96
  68.3 2.0 %reshape_reshape_squeeze.13 = bf16[640,12,64]{0,2,1:T(8,128)(2,1)} reshape(bf16[5,1,128,768]{2,0,3,1:T(8,128)(2,1)S(1)} %copy.19) | data formatting | bytes 1966080 | tf_op jit(solution)/shard_map/reshape;reshape;squeeze | solution.py:29
  70.3 2.0 %copy.17 = bf16[5,1,128,768]{2,0,3,1:T(8,128)(2,1)S(1)} copy(bf16[5,1,128,768]{3,2,1,0:T(8,128)(2,1)} %get-tuple-element.8) | data formatting | bytes 1966080 | tf_op jit(solution)/shard_map/slice | solution.py:99
  72.3 2.0 %reshape_reshape_squeeze.12 = bf16[640,12,64]{0,2,1:T(8,128)(2,1)} reshape(bf16[5,1,128,768]{2,0,3,1:T(8,128)(2,1)S(1)} %copy.17) | data formatting | bytes 1966080 | tf_op jit(solution)/shard_map/reshape;reshape;squeeze | solution.py:30
  74.4 2.0 %copy.22 = bf16[5,1,128,768]{2,0,3,1:T(8,128)(2,1)S(1)} copy(bf16[5,1,128,768]{3,2,1,0:T(8,128)(2,1)} %get-tuple-element.6) | data formatting | bytes 1966080 | tf_op jit(solution)/shard_map/slice | solution.py:96
  76.4 2.0 %reshape_reshape_squeeze.15 = bf16[640,12,64]{0,2,1:T(8,128)(2,1)} reshape(bf16[5,1,128,768]{2,0,3,1:T(8,128)(2,1)S(1)} %copy.22) | data formatting | bytes 1966080 | tf_op jit(solution)/shard_map/reshape;reshape;squeeze | solution.py:29
  78.4 2.0 %copy.20 = bf16[5,1,128,768]{2,0,3,1:T(8,128)(2,1)S(1)} copy(bf16[5,1,128,768]{3,2,1,0:T(8,128)(2,1)} %get-tuple-element.7) | data formatting | bytes 1966080 | tf_op jit(solution)/shard_map/slice | solution.py:99
  80.4 2.0 %reshape_reshape_squeeze.14 = bf16[640,12,64]{0,2,1:T(8,128)(2,1)} reshape(bf16[5,1,128,768]{2,0,3,1:T(8,128)(2,1)S(1)} %copy.20) | data formatting | bytes 1966080 | tf_op jit(solution)/shard_map/reshape;reshape;squeeze | solution.py:30
  82.4 4.5 %fusion.55 = (f32[12,128]{1,0:T(8,128)S(1)}, f32[12,128,640]{2,1,0:T(8,128)}) fusion(pred[640]{0:T(1024)(128)(4,1)S(1)} %broadcast_bitcast_fusion, bf16[128,12,64]{0,2,1:T(8,128)(2,1)S(1)} %bitcast.102, bf16[640,12,64]{0,2,1:T(8,128)(2,1)} %reshape_reshape_squeeze.13), kind=kOutput, calls=%fused_computation.80 | convolution fusion | flops 129761920 | bytes 5118592 | tf_op jit(solution)/shard_map/sub | solution.py:36
  87.0 4.3 %fusion.54 = (f32[12,128]{1,0:T(8,128)S(1)}, f32[12,128,640]{2,1,0:T(8,128)}) fusion(pred[640]{0:T(1024)(128)(4,1)S(1)} %broadcast_bitcast_fusion, bf16[128,12,64]{0,2,1:T(8,128)(2,1)} %bitcast.103, bf16[640,12,64]{0,2,1:T(8,128)(2,1)S(1)} %copy-done.4), kind=kOutput, calls=%fused_computation.79 | convolution fusion | flops 129761920 | bytes 5118592 | tf_op jit(solution)/shard_map/sub | solution.py:36
  91.3 3.2 %fusion.33 = f32[12,64,128]{2,1,0:T(8,128)S(1)} fusion(bf16[640,12,64]{0,2,1:T(8,128)(2,1)S(1)} %copy-done.2, f32[12,128,640]{2,1,0:T(8,128)} %get-tuple-element.18, f32[12,128]{1,0:T(8,128)S(1)} %get-tuple-element.17), kind=kOutput, calls=%fused_computation.40 | convolution fusion | flops 127991808 | bytes 5314560 | tf_op jit(solution)/shard_map/hsk,khd->shd/dot_general | solution.py:38
  97.2 2.0 %convolution_add_fusion = f32[128,3072]{1,0:T(8,128)} fusion(f32[128,3072]{1,0:T(8,128)S(1)} %fusion.43, bf16[768,3072]{1,0:T(8,128)(2,1)S(1)} %bitcast.95, f32[128,768]{0,1:T(8,128)S(1)} %fusion.37), kind=kOutput, calls=%fused_computation.13 | convolution fusion | flops 604766208 | bytes 8257536 | tf_op jit(solution)/shard_map/dot_general | solution.py:116
  99.8 23.9 %reduce-scatter.2.cloned.1.call-done = f32[128,1536]{1,0:T(8,128)} async-done(((f32[128,3072]{1,0:T(8,128)}), f32[128,1536]{1,0:T(8,128)}) %reduce-scatter.2.cloned.1.call-update) | async-done | bytes 786448 | tf_op jit(solution)/shard_map/reduce_scatter | solution.py:119
  123.7 2.5 %fusion.35 = bf16[1,128,1536]{2,1,0:T(8,128)(2,1)S(1)} fusion(f32[128,1536]{1,0:T(8,128)} %reduce-scatter.2.cloned.1.call-done, bf16[1,128,1536]{2,1,0:T(8,128)(2,1)S(1)} %copy-done.1, f32[]{:T(128)} %get-tuple-element.19, f32[]{:T(128)} %get-tuple-element.20), kind=kLoop, calls=%fused_computation.48 | loop fusion | flops 983040 | bytes 1572872 | tf_op jit(solution)/shard_map/broadcast_in_dim | solution.py:122
  126.2 1.9 %collective-permute-start.4 = (bf16[1,128,1536]{2,1,0:T(8,128)(2,1)S(1)}, bf16[1,128,1536]{2,1,0:T(8,128)(2,1)S(1)}, u32[]{:S(2)}, u32[]{:S(2)}) collective-permute-start(bf16[1,128,1536]{2,1,0:T(8,128)(2,1)S(1)} %fusion.35), channel_id=1, source_target_pairs={{0,2},{2,4},{4,6},{6,8},{8,10},{10,12},{12,14},{14,16},{16,18},{18... | collective-permute-start | bytes 1179656 | tf_op jit(solution)/shard_map/ppermute | solution.py:23
  128.1 13.1 %collective-permute-done.4 = bf16[1,128,1536]{2,1,0:T(8,128)(2,1)S(1)} collective-permute-done((bf16[1,128,1536]{2,1,0:T(8,128)(2,1)S(1)}, bf16[1,128,1536]{2,1,0:T(8,128)(2,1)S(1)}, u32[]{:S(2)}, u32[]{:S(2)}) %collective-permute-start.4) | collective-permute-done | bytes 393248 | tf_op jit(solution)/shard_map/ppermute | solution.py:23
  (55 shorter events, 14.1 us)
Async XLA Ops:
  6.5 1.3 copy-start
  6.5 5.8 %copy-start.5 = (f32[2,2,3072]{2,1,0:T(2,128)S(1)}, f32[2,2,3072]{2,1,0:T(2,128)}, u32[]{:S(2)}) copy-start(f32[2,2,3072]{2,1,0:T(2,128)} %param.15) | copy-start | bytes 147460
  6.5 117.2 %reduce-scatter.2.cloned.1.call-start = ((), (), s32[]{:S(2)}) async-start(), calls=%async_computation.1 | async-start | bytes 2359296 | tf_op jit(solution)/shard_map/reduce_scatter | solution.py:119
  19.1 38.7 %collective-permute-start = (bf16[2,256,768]{2,1,0:T(8,128)(2,1)S(1)}, bf16[2,256,768]{2,1,0:T(8,128)(2,1)}, u32[]{:S(2)}, u32[]{:S(2)}) collective-permute-start(bf16[2,256,768]{2,1,0:T(8,128)(2,1)S(1)} %bitcast.98), channel_id=1, source_target_pairs={{0,4},{2,6},{4,8},{6,10},{8,12},{10,14},{12,16},{14,18},{16,20},{1... | collective-permute-start | bytes 2359304 | tf_op jit(solution)/shard_map/ppermute | solution.py:17
  24.8 37.0 %collective-permute-start.1 = (bf16[2,256,768]{2,1,0:T(8,128)(2,1)S(1)}, bf16[2,256,768]{2,1,0:T(8,128)(2,1)}, u32[]{:S(2)}, u32[]{:S(2)}) collective-permute-start(bf16[2,256,768]{2,1,0:T(8,128)(2,1)S(1)} %bitcast.99), channel_id=1, source_target_pairs={{0,2},{2,4},{4,6},{6,8},{8,10},{10,12},{12,14},{14,16},{16,18},{18... | collective-permute-start | bytes 2359304 | tf_op jit(solution)/shard_map/ppermute | solution.py:17
  29.1 34.0 %collective-permute-start.2 = (bf16[2,256,768]{2,1,0:T(8,128)(2,1)S(1)}, bf16[2,256,768]{2,1,0:T(8,128)(2,1)}, u32[]{:S(2)}, u32[]{:S(2)}) collective-permute-start(bf16[2,256,768]{2,1,0:T(8,128)(2,1)S(1)} %bitcast.100), channel_id=1, source_target_pairs={{2,0},{4,2},{6,4},{8,6},{10,8},{12,10},{14,12},{16,14},{18,16},{20... | collective-permute-start | bytes 2359304 | tf_op jit(solution)/shard_map/ppermute | solution.py:17
  30.4 33.9 %collective-permute-start.3 = (bf16[2,256,768]{2,1,0:T(8,128)(2,1)S(1)}, bf16[2,256,768]{2,1,0:T(8,128)(2,1)S(1)}, u32[]{:S(2)}, u32[]{:S(2)}) collective-permute-start(bf16[2,256,768]{2,1,0:T(8,128)(2,1)S(1)} %bitcast.101), channel_id=1, source_target_pairs={{4,0},{6,2},{8,4},{10,6},{12,8},{14,10},{16,12},{18,14},{20,16},{2... | collective-permute-start | bytes 2359304 | tf_op jit(solution)/shard_map/ppermute | solution.py:17
  82.4 4.5 %copy-start.4 = (bf16[640,12,64]{0,2,1:T(8,128)(2,1)S(1)}, bf16[640,12,64]{0,2,1:T(8,128)(2,1)}, u32[]{:S(2)}) copy-start(bf16[640,12,64]{0,2,1:T(8,128)(2,1)} %reshape_reshape_squeeze.15) | copy-start | bytes 2949124
  87.0 4.3 %copy-start.2 = (bf16[640,12,64]{0,2,1:T(8,128)(2,1)S(1)}, bf16[640,12,64]{0,2,1:T(8,128)(2,1)}, u32[]{:S(2)}) copy-start(bf16[640,12,64]{0,2,1:T(8,128)(2,1)} %reshape_reshape_squeeze.12) | copy-start | bytes 2949124
  91.3 3.3 %copy-start.3 = (bf16[640,12,64]{0,2,1:T(8,128)(2,1)S(1)}, bf16[640,12,64]{0,2,1:T(8,128)(2,1)}, u32[]{:S(2)}) copy-start(bf16[640,12,64]{0,2,1:T(8,128)(2,1)} %reshape_reshape_squeeze.14) | copy-start | bytes 2949124
  91.3 3.6 %copy-start.8 = (f32[12,128,640]{2,1,0:T(8,128)S(1)}, f32[12,128,640]{2,1,0:T(8,128)}, u32[]{:S(2)}) copy-start(f32[12,128,640]{2,1,0:T(8,128)} %get-tuple-element.16) | copy-start | bytes 11796484
  91.3 4.9 %slice-start = ((s8[4718592]{0:T(1024)(128)(4,1)}), s8[4194304]{0:T(1024)(128)(4,1)S(1)}, s32[]{:S(2)}) async-start(s8[4718592]{0:T(1024)(128)(4,1)} %bitcast.94), calls=%async_computation.2 | async-start | bytes 8388608
  94.9 1.5 %slice-start.1 = ((s8[4718592]{0:T(1024)(128)(4,1)}), s8[524288]{0:T(1024)(128)(4,1)S(1)}, s32[]{:S(2)}) async-start(s8[4718592]{0:T(1024)(128)(4,1)} %bitcast.94), calls=%async_computation.3 | async-start | bytes 1048576
  97.2 2.1 %copy-start.6 = (f32[50]{0:T(128)S(1)}, f32[50]{0:T(128)}, u32[]{:S(2)}) copy-start(f32[50]{0:T(128)} %param.19) | copy-start | bytes 604
  97.2 2.1 %copy-start.7 = (f32[50]{0:T(128)S(1)}, f32[50]{0:T(128)}, u32[]{:S(2)}) copy-start(f32[50]{0:T(128)} %param.18) | copy-start | bytes 604
  97.2 26.5 %copy-start.1 = (bf16[1,128,1536]{2,1,0:T(8,128)(2,1)S(1)}, bf16[1,128,1536]{2,1,0:T(8,128)(2,1)}, u32[]{:S(2)}) copy-start(bf16[1,128,1536]{2,1,0:T(8,128)(2,1)} %param.10) | copy-start | bytes 1179652
  126.2 15.0 %collective-permute-start.4 = (bf16[1,128,1536]{2,1,0:T(8,128)(2,1)S(1)}, bf16[1,128,1536]{2,1,0:T(8,128)(2,1)S(1)}, u32[]{:S(2)}, u32[]{:S(2)}) collective-permute-start(bf16[1,128,1536]{2,1,0:T(8,128)(2,1)S(1)} %fusion.35), channel_id=1, source_target_pairs={{0,2},{2,4},{4,6},{6,8},{8,10},{10,12},{12,14},{14,16},{16,18},{18... | collective-permute-start | bytes 1179656 | tf_op jit(solution)/shard_map/ppermute | solution.py:23
Sparse Core Ops, SparseCore 0:
  99.3 24.3 reduce-scatter.1
where the time goes:
time: 149 us
  waiting for transfers between devices  59.8 us (40%)
  matrix products  26.8 us (18%)
  local copies, waits for them, and re-layouts  24.9 us (17%)
  between operations  15.7 us (11%)
  starting transfers between devices  14.4 us (10%)
  other arithmetic  4.4 us (3%)
  blocking collectives  2.7 us (2%)
    reduce_scatter x1, waiting for transfers between devices, on_device(): lax.psum_scatter(partial_value, 'tp', scatter_dimension=1, tiled=True)  23.9 us
    ppermute x4, waiting for transfers between devices, passed_along(): lax.ppermute(value, axis, [(source, source + steps) for source in range(i...  22.8 us
    ppermute x1, waiting for transfers between devices, shifted(): return lax.ppermute(value, axis, pairs)  13.1 us
    ppermute x4, starting transfers between devices, passed_along(): lax.ppermute(value, axis, [(source, source + steps) for source in range(i...  12.5 us
    sub x2, matrix products, attend(): expon = jnp.exp(scores - top)  8.84 us
    dot_general x1, matrix products, on_device(): jnp.einsum('rd,cde->cre', normed, w_qkv[1:], preferred_element_type=jnp.f...  6.31 us
    slice x3, local copies, waits for them, and re-layouts, on_device(): stacked[:, 0, rows_from:rows_from + tokens]  6 us
    unnamed x28, local copies, waits for them, and re-layouts  5.72 us
  transfers between devices with their start and end apart: 6, of which 4 were waited for; matrix products, arithmetic and copies ran while one was open for 6% of the time, Pallas kernels for 0%

commit v1 on v0

v1 whole, which is shorter than its diff:
```python
import functools

import jax
import jax.numpy as jnp
from jax import lax
from jax.experimental import pallas as pl
from jax.experimental.pallas import tpu as pltpu
from jax.sharding import PartitionSpec as P

HDIM = 64
REACH = 2
SPAN = 2 * REACH + 1
epsilon = 1e-06
guidance = 6.0
MESH = pl.DeviceIdType.MESH

CHUNKS = 4
TILE = 256
OUT_TILE = 512
ROWS = 16

OWN, X, Y, Z, R = range(5)


def kernel(
    n,
    step_ref,
    back_ref,
    ahead_ref,
    keep_ref,
    noise_ref,
    level_ref,
    text_ref,
    latent_hbm,
    wqkv_hbm,
    wout_hbm,
    out_ref,
    frames,
    mods,
    wqkv,
    wout,
    nbuf,
    qbuf,
    kbuf,
    vbuf,
    mix,
    give,
    take,
    stage,
    own_sem,
    wq_sem,
    wo_sem,
    mod_send,
    mod_recv,
    par_send,
    par_recv,
    xy_send,
    z_send,
    r_send,
    ici_recv,
    give_send,
    take_recv,
    roll_send,
    roll_recv,
):
    p = lax.axis_index("queue")
    t = lax.axis_index("tp")
    o = 1 - t
    tokens, half = out_ref.shape
    cols = wqkv.shape[2]
    rows_c = tokens // CHUNKS
    low = lax.rem(p, 2)
    mid = lax.rem(p // 2, 2)
    xp = p + 1 - 2 * low
    yp = p + 2 - 4 * mid
    zdir = 1 - 2 * mid
    zto = p + 4 * zdir
    zfrom = p - 4 * zdir
    has_zto = (zto >= 0) & (zto < n)
    has_zfrom = (zfrom >= 0) & (zfrom < n)
    relays_y = low == mid
    relays_z = low != mid
    has_r = relays_z | has_zfrom
    following = lax.rem(p + 1, n)
    preceding = lax.rem(p + n - 1, n)
    offsets = (0, 1 - 2 * low, 2 - 4 * mid, 4 * mid - 2, 2 * low - 1)

    own_copy = pltpu.make_async_copy(latent_hbm.at[0], frames.at[OWN, t], own_sem)
    own_copy.start()
    w_copies = [
        pltpu.make_async_copy(wqkv_hbm.at[i], wqkv.at[i], wq_sem.at[i]) for i in range(3)
    ]
    for i in range(3):
        w_copies[i].start()
    wo_copy = pltpu.make_async_copy(wout_hbm, wout, wo_sem)
    wo_copy.start()
    step = step_ref[0]
    mods[REACH] = level_ref[step]

    barrier = pltpu.get_barrier_semaphore()

    def greet(q, tp):
        pl.semaphore_signal(barrier, inc=1, device_id=(q, tp), device_id_type=MESH)

    greet(p, o)
    greet(xp, t)
    greet(yp, t)
    greet(following, t)
    greet(preceding, t)
    optional = [
        (has_zto, zto),
        (has_zfrom, zfrom),
        (p + 1 < n, p + 1),
        (p >= 1, p - 1),
        (p + 2 < n, p + 2),
        (p >= 2, p - 2),
    ]
    for cond, q in optional:
        @pl.when(cond)
        def _(q=q):
            greet(q, t)
    pl.semaphore_wait(barrier, 5 + sum(cond.astype(jnp.int32) for cond, _ in optional))
    own_copy.wait()

    def remote(src, dst, ssem, rsem, q, tp):
        return pltpu.make_async_remote_copy(
            src_ref=src, dst_ref=dst, send_sem=ssem, recv_sem=rsem,
            device_id=(q, tp), device_id_type=MESH,
        )

    def piece(slot, side, c):
        return frames.at[slot, side, pl.ds(c * rows_c, rows_c)]

    def to_partner(slot, c):
        return remote(piece(slot, t, c), piece(slot, t, c),
                      par_send.at[slot, c], par_recv.at[slot, c], p, o)

    def from_partner(slot, c):
        return remote(piece(slot, o, c), piece(slot, o, c),
                      par_send.at[slot, c], par_recv.at[slot, c], p, o)

    def own_to(slot, c):
        return remote(piece(OWN, t, c), piece(slot, t, c),
                      xy_send.at[slot - X, c], ici_recv.at[slot - X, c],
                      xp if slot == X else yp, t)

    def y_to_z(c):
        return remote(piece(Y, t, c), piece(Z, t, c),
                      z_send.at[c], ici_recv.at[Z - X, c], zto, t)

    def slot_to_r(slot, c):
        return remote(piece(slot, t, c), piece(R, t, c),
                      r_send.at[c], ici_recv.at[R - X, c], xp, t)

    def mod_to(d):
        return remote(mods.at[REACH], mods.at[REACH - d],
                      mod_send.at[REACH + d], mod_recv.at[REACH - d], p + d, t)

    for c in range(CHUNKS):
        own_to(Y, c).start()
        own_to(X, c).start()
        to_partner(OWN, c).start()
    for d in (1, -1, 2, -2):
        @pl.when((p + d >= 0) & (p + d < n))
        def _(d=d):
            mod_to(d).start()

    def arrived(slot, c):
        remote(piece(slot, t, c), piece(slot, t, c), xy_send.at[0, c],
               ici_recv.at[slot - X, c], xp, t).wait_recv()

    def relay_x(c):
        arrived(X, c)
        to_partner(X, c).start()

    def relay_y(c):
        arrived(Y, c)

        @pl.when(has_zto)
        def _():
            y_to_z(c).start()

        @pl.when(relays_y)
        def _():
            slot_to_r(Y, c).start()
        to_partner(Y, c).start()

    def relay_z(c):
        @pl.when(has_zfrom)
        def _():
            arrived(Z, c)

            @pl.when(relays_z)
            def _():
                slot_to_r(Z, c).start()
            to_partner(Z, c).start()

    def relay_r(c):
        @pl.when(has_r)
        def _():
            arrived(R, c)
            to_partner(R, c).start()

    def clear(slot):
        frames[slot] = jnp.zeros(frames.shape[1:], frames.dtype)

    @pl.when(jnp.logical_not(has_zfrom))
    def _():
        clear(Z)

    @pl.when(jnp.logical_not(has_r))
    def _():
        clear(R)

    for d in (1, -1, 2, -2):
        @pl.when((p + d < 0) | (p + d >= n))
        def _(d=d):
            mods[REACH + d] = jnp.zeros(mods.shape[1:], mods.dtype)

    def normalize(slot, base):
        modulation = mods[REACH + offsets[slot]]
        text = text_ref[...]
        shift = [modulation[0:1] + text[b, 0:1] for b in range(2)]
        scale = [1.0 + (modulation[1:2] + text[b, 1:2]) for b in range(2)]

        def body(i, carry):
            at = pl.ds(pl.multiple_of(i * ROWS, ROWS), ROWS)
            parts = [frames[slot, h, at, :].astype(jnp.float32) for h in range(2)]
            total = sum(jnp.sum(v, axis=-1, keepdims=True) for v in parts)
            mean = total * (1.0 / (2 * half))
            parts = [v - mean for v in parts]
            spread = sum(jnp.sum(v * v, axis=-1, keepdims=True) for v in parts)
            inv = lax.rsqrt(spread * (1.0 / (2 * half)) + epsilon)
            for h in range(2):
                span = slice(h * half, (h + 1) * half)
                unit = parts[h] * inv
                for b in range(2):
                    row = pl.ds(pl.multiple_of(base + b * tokens + i * ROWS, ROWS), ROWS)
                    nbuf[row, span] = (
                        unit * scale[b][:, span] + shift[b][:, span]
                    ).astype(nbuf.dtype)
            return carry

        lax.fori_loop(0, tokens // ROWS, body, 0)

    def project(kind, slots):
        m = 2 * tokens * len(slots)

        def body(j, carry):
            at = pl.ds(pl.multiple_of(j * TILE, TILE), TILE)
            res = jnp.dot(
                nbuf[0:m, :], wqkv[kind, :, at], preferred_element_type=jnp.float32
            )
            if kind == 0:
                res = res * HDIM ** (-0.5)
            res = res.astype(jnp.bfloat16)
            for k, slot in enumerate(slots):
                for b in range(2):
                    rows = res[(2 * k + b) * tokens : (2 * k + b + 1) * tokens]
                    if kind == 0:
                        qbuf[b, :, at] = rows
                    else:
                        dst = kbuf if kind == 1 else vbuf
                        dst[b, slot * tokens : (slot + 1) * tokens, at] = rows
            return carry

        lax.fori_loop(0, cols // TILE, body, 0)

    def mod_arrives(d):
        @pl.when((p + d >= 0) & (p + d < n))
        def _():
            remote(mods.at[REACH + d], mods.at[REACH + d], mod_send.at[REACH],
                   mod_recv.at[REACH + d], p, o).wait_recv()

    for c in range(CHUNKS):
        from_partner(OWN, c).wait_recv()
    normalize(OWN, 0)
    w_copies[0].wait()
    project(0, (OWN,))
    relay_y(0)
    relay_x(0)
    w_copies[1].wait()
    project(1, (OWN,))
    relay_y(1)
    relay_x(1)
    w_copies[2].wait()
    project(2, (OWN,))
    for d in (1, -1, 2, -2):
        mod_arrives(d)
    for c in range(2, CHUNKS):
        relay_y(c)
        relay_z(c - 2)
        relay_x(c)
    for c in range(CHUNKS):
        from_partner(X, c).wait_recv()
    normalize(X, 0)
    for c in range(CHUNKS):
        from_partner(Y, c).wait_recv()
    relay_r(0)
    normalize(Y, 2 * tokens)
    relay_z(2)
    project(1, (X, Y))
    relay_z(3)
    relay_r(1)
    project(2, (X, Y))
    relay_r(2)

    def slot_full(slot, cond):
        @pl.when(cond)
        def _():
            for c in range(CHUNKS):
                from_partner(slot, c).wait_recv()

    slot_full(Z, has_zfrom)
    normalize(Z, 0)
    relay_r(3)
    slot_full(R, has_r)
    normalize(R, 2 * tokens)
    project(1, (Z, R))
    project(2, (Z, R))

    lane = lax.broadcasted_iota(jnp.int32, (1, SPAN * tokens), 1) // tokens
    bias = jnp.zeros((1, SPAN * tokens), jnp.float32)
    for slot in range(SPAN):
        off = offsets[slot]
        target = p + off
        ok = (off >= -back_ref[0]) & (off <= ahead_ref[0]) & (target >= 0) & (target < n)
        bias = jnp.where(lane == slot, jnp.where(ok, 0.0, -1e30), bias)
    pair = 2 * HDIM
    first = lax.broadcasted_iota(jnp.int32, (1, pair), 1) < HDIM

    def heads(j, carry):
        at = pl.ds(pl.multiple_of(j * pair, pair), pair)
        outs = []
        for b in range(2):
            q = qbuf[b, :, at]
            zero = jnp.zeros_like(q)
            both = jnp.concatenate([jnp.where(first, q, zero), jnp.where(first, zero, q)], axis=0)
            scores = lax.dot_general(
                both, kbuf[b, :, at], (((1,), (1,)), ((), ())),
                preferred_element_type=jnp.float32,
            ) + bias
            top = jnp.max(scores, axis=-1, keepdims=True)
            expon = jnp.exp(scores - top)
            inv = 1.0 / jnp.sum(expon, axis=-1, keepdims=True)
            probs = (expon * inv).astype(jnp.bfloat16)
            att = jnp.dot(probs, vbuf[b, :, at], preferred_element_type=jnp.float32)
            att = jnp.where(first, att[:tokens], att[tokens:])
            outs.append(att.astype(jnp.bfloat16).astype(jnp.float32))
        mixture = outs[1] + guidance * (outs[0] - outs[1])
        upper = mixture.astype(jnp.bfloat16)
        mix[0:tokens, at] = upper
        mix[tokens : 2 * tokens, at] = (mixture - upper.astype(jnp.float32)).astype(jnp.bfloat16)
        return carry

    lax.fori_loop(0, cols // pair, heads, 0)

    wo_copy.wait()
    tiles = half // OUT_TILE

    def partial(side, j):
        at = pl.ds(pl.multiple_of(side * half + j * OUT_TILE, OUT_TILE), OUT_TILE)
        res = jnp.dot(mix[...], wout[:, at], preferred_element_type=jnp.float32)
        return res[:tokens] + res[tokens:]

    def hand(j):
        return remote(give.at[j], take.at[j], give_send.at[j], take_recv.at[j], p, o)

    def rolled(j):
        return remote(stage.at[j], out_ref.at[:, j * OUT_TILE : (j + 1) * OUT_TILE],
                      roll_send.at[j], roll_recv.at[j], following, t)

    for j in range(tiles):
        give[j] = partial(o, j)
        hand(j).start()
    keep = keep_ref[step]
    noise = noise_ref[step]
    for j in range(tiles):
        mine = partial(t, j)
        hand(j).wait_recv()
        guided = mine + take[j]
        current = frames[OWN, t, :, j * OUT_TILE : (j + 1) * OUT_TILE].astype(jnp.float32)
        stage[j] = (keep * current - noise * guided).astype(stage.dtype)
        rolled(j).start()

    for c in range(CHUNKS):
        own_to(X, c).wait_send()
        own_to(Y, c).wait_send()
        for slot in (OWN, X, Y):
            to_partner(slot, c).wait_send()

        @pl.when(has_zto)
        def _(c=c):
            y_to_z(c).wait_send()

        @pl.when(has_zfrom)
        def _(c=c):
            to_partner(Z, c).wait_send()

        @pl.when(relays_y | has_zfrom)
        def _(c=c):
            slot_to_r(Y, c).wait_send()

        @pl.when(has_r)
        def _(c=c):
            to_partner(R, c).wait_send()
    for d in (1, -1, 2, -2):
        @pl.when((p + d >= 0) & (p + d < n))
        def _(d=d):
            mod_to(d).wait_send()
    for j in range(tiles):
        hand(j).wait_send()
        rolled(j).wait()


def on_device(
    latent, step_index, back_reach, ahead_reach, level_mod, text_mod,
    w_qkv, w_out, keep_coef, noise_coef,
):
    n = lax.axis_size("queue")
    _, tokens, half = latent.shape
    cols = w_qkv.shape[2]
    tiles = half // OUT_TILE
    dma = pltpu.SemaphoreType.DMA
    bf16, f32 = jnp.bfloat16, jnp.float32
    smem = pl.BlockSpec(memory_space=pltpu.SMEM)
    vmem = pl.BlockSpec(memory_space=pltpu.VMEM)
    hbm = pl.BlockSpec(memory_space=pl.ANY)
    out = pl.pallas_call(
        functools.partial(kernel, n),
        out_shape=jax.ShapeDtypeStruct((tokens, half), bf16),
        in_specs=[smem] * 5 + [vmem] * 2 + [hbm] * 3,
        out_specs=vmem,
        scratch_shapes=[
            pltpu.VMEM((SPAN, 2, tokens, half), bf16),
            pltpu.VMEM((SPAN, 2, 2 * half), f32),
            pltpu.VMEM(w_qkv.shape, bf16),
            pltpu.VMEM(w_out.shape, bf16),
            pltpu.VMEM((4 * tokens, 2 * half), bf16),
            pltpu.VMEM((2, tokens, cols), bf16),
            pltpu.VMEM((2, SPAN * tokens, cols), bf16),
            pltpu.VMEM((2, SPAN * tokens, cols), bf16),
            pltpu.VMEM((2 * tokens, cols), bf16),
            pltpu.VMEM((tiles, tokens, OUT_TILE), f32),
            pltpu.VMEM((tiles, tokens, OUT_TILE), f32),
            pltpu.VMEM((tiles, tokens, OUT_TILE), bf16),
            dma, dma((3,)), dma,
            dma((SPAN,)), dma((SPAN,)),
            dma((SPAN, CHUNKS)), dma((SPAN, CHUNKS)),
            dma((2, CHUNKS)), dma((CHUNKS,)), dma((CHUNKS,)), dma((4, CHUNKS)),
            dma((tiles,)), dma((tiles,)), dma((tiles,)), dma((tiles,)),
        ],
        compiler_params=pltpu.CompilerParams(
            collective_id=0, has_side_effects=True, vmem_limit_bytes=62 * 1024 * 1024
        ),
    )(
        step_index, back_reach, ahead_reach, keep_coef, noise_coef, level_mod, text_mod,
        latent, w_qkv, w_out,
    )
    return out[None]


def solution(mesh):
    return jax.shard_map(
        on_device,
        mesh=mesh,
        in_specs=(
            P("queue", None, "tp"),
            P("queue"),
            P("queue"),
            P("queue"),
            P(),
            P(),
            P(None, None, "tp"),
            P("tp", None),
            P(),
            P(),
        ),
        out_specs=P("queue", None, "tp"),
        check_vma=False,
    )
```

time: 149 us -> 71.1 us (0.48)
  Pallas kernels: 0 us -> 67.2 us
  waiting for transfers between devices: 59.8 us -> 0 us
  matrix products: 26.8 us -> 0 us
  local copies, waits for them, and re-layouts: 24.9 us -> 1.77 us
  starting transfers between devices: 14.4 us -> 0 us
  between operations: 15.7 us -> 1.95 us
  other arithmetic: 4.4 us -> 0 us
  blocking collectives: 2.7 us -> 0 us
    pallas_call x0 -> x1, Pallas kernels: none -> 67.2 us  [on_device(): pl.pallas_call(functools.partial(kernel, n), out_shape=jax.ShapeDtypeStru...]
    ppermute x5 -> x0, waiting for transfers between devices: 35.9 us -> none  [the longest x4 22.8 us: passed_along(): lax.ppermute(value, axis, [(source, source + steps) for source in range(i...]
    reduce_scatter x1 -> x0, waiting for transfers between devices: 23.9 us -> none  [on_device(): lax.psum_scatter(partial_value, 'tp', scatter_dimension=1, tiled=True)]
    dot_general x7 -> x0, matrix products: 18 us -> none  [the longest x1 6.31 us: on_device(): jnp.einsum('rd,cde->cre', normed, w_qkv[1:], preferred_element_type=jnp.f...]
    ppermute x5 -> x0, starting transfers between devices: 14.4 us -> none  [the longest x4 12.5 us: passed_along(): lax.ppermute(value, axis, [(source, source + steps) for source in range(i...]
    slice x9 -> x0, local copies, waits for them, and re-layouts: 11.1 us -> none  [the longest x3 6 us: on_device(): stacked[:, 0, rows_from:rows_from + tokens]]
    sub x2 -> x0, matrix products: 8.84 us -> none  [attend(): expon = jnp.exp(scores - top)]
    another operation x5 -> x0, local copies, waits for them, and re-layouts: 8.04 us -> none  [the longest x2 4 us: attend(): value_heads = value_block.reshape(value_block.shape[0], local_heads, HDIM)]
  transfers between devices with their start and end apart: 6 -> 0, of which waited for: 4 -> 0; matrix products, arithmetic and copies ran while one was open for 6% -> 0% of each run, Pallas kernels for 0% -> 0%
where the time goes in v1:
time: 71.1 us; the launch traced here: 70.9 us
  Pallas kernels  67.2 us (95%)
  between operations  1.95 us (3%)
  local copies, waits for them, and re-layouts  1.77 us (2%)
    pallas_call x1, Pallas kernels, on_device(): pl.pallas_call(functools.partial(kernel, n), out_shape=jax.ShapeDtypeStru...  67.2 us
    unnamed x1, local copies, waits for them, and re-layouts  1.77 us

profile of v1, /device:TPU:0, one launch (start us, length us, event | category | flops | bytes accessed | tf_op | source)
XLA Modules:
  0.0 70.9 jit_solution(10338772931932274929)
XLA Ops:
  1.9 67.2 %shard_map.100 = bf16[128,1536]{1,0:T(8,128)(2,1)} custom-call(s32[1]{0:T(128)S(6)} %copy.12.step_ref, s32[1]{0:T(128)S(6)} %copy.13.back_ref, s32[1]{0:T(128)S(6)} %copy.14.ahead_ref, f32[50]{0:T(128)} %keep_ref.1, f32[50]{0:T(128)} %noise_ref.1, f32[50,2,3072]{2,1,0:T(2,128)} %level_ref.1, f32[2,2,3072]{2,1,0:T(2,128)} %text_ref.1, ...), custom_call_target="tpu_custom_call" | custom-call | tf_op jit(solution)/shard_map/pallas_call | solution.py:429
  69.1 1.8 %copy.15 = bf16[1,128,1536]{2,1,0:T(8,128)(2,1)} copy(bf16[1,128,1536]{2,1,0:T(8,128)(2,1)} %bitcast.1) | data formatting | bytes 786432

commit v2 on v1

--- a/solution.py
+++ b/solution.py
@@ -46,7 +46,8 @@
     mix,
     give,
     take,
-    stage,
+    mix_out,
+    coefs,
     own_sem,
     wq_sem,
     wo_sem,
@@ -62,6 +63,10 @@
     take_recv,
     roll_send,
     roll_recv,
+    coef_send,
+    coef_recv,
+    wrap_send,
+    wrap_recv,
 ):
     p = lax.axis_index("queue")
     t = lax.axis_index("tp")
@@ -96,6 +101,24 @@
     wo_copy.start()
     step = step_ref[0]
     mods[REACH] = level_ref[step]
+    coefs[0, 0] = jnp.full(coefs.shape[2:], keep_ref[step], jnp.float32)
+    coefs[0, 1] = jnp.full(coefs.shape[2:], noise_ref[step], jnp.float32)
+
+    def clear(slot):
+        frames[slot] = jnp.zeros(frames.shape[1:], frames.dtype)
+
+    @pl.when(jnp.logical_not(has_zfrom))
+    def _():
+        clear(Z)
+
+    @pl.when(jnp.logical_not(has_r))
+    def _():
+        clear(R)
+
+    for d in (1, -1, 2, -2):
+        @pl.when((p + d < 0) | (p + d >= n))
+        def _(d=d):
+            mods[REACH + d] = jnp.zeros(mods.shape[1:], mods.dtype)
 
     barrier = pltpu.get_barrier_semaphore()
 
@@ -164,6 +187,14 @@
         @pl.when((p + d >= 0) & (p + d < n))
         def _(d=d):
             mod_to(d).start()
+    coef_copy = remote(coefs.at[0], coefs.at[1], coef_send, coef_recv, following, t)
+    coef_copy.start()
+
+    wrap_copy = remote(frames.at[OWN, t], frames.at[R, t], wrap_send, wrap_recv, following, t)
+
+    @pl.when(p == n - 1)
+    def _():
+        wrap_copy.start()
 
     def arrived(slot, c):
         remote(piece(slot, t, c), piece(slot, t, c), xy_send.at[0, c],
@@ -200,22 +231,6 @@
         def _():
             arrived(R, c)
             to_partner(R, c).start()
-
-    def clear(slot):
-        frames[slot] = jnp.zeros(frames.shape[1:], frames.dtype)
-
-    @pl.when(jnp.logical_not(has_zfrom))
-    def _():
-        clear(Z)
-
-    @pl.when(jnp.logical_not(has_r))
-    def _():
-        clear(R)
-
-    for d in (1, -1, 2, -2):
-        @pl.when((p + d < 0) | (p + d >= n))
-        def _(d=d):
-            mods[REACH + d] = jnp.zeros(mods.shape[1:], mods.dtype)
 
     def normalize(slot, base):
         modulation = mods[REACH + offsets[slot]]
@@ -241,7 +256,7 @@
                     ).astype(nbuf.dtype)
             return carry
 
-        lax.fori_loop(0, tokens // ROWS, body, 0)
+        lax.fori_loop(0, tokens // ROWS, body, 0, unroll=2)
 
     def project(kind, slots):
         m = 2 * tokens * len(slots)
@@ -315,6 +330,10 @@
     normalize(Z, 0)
     relay_r(3)
     slot_full(R, has_r)
+
+    @pl.when(p == 0)
+    def _():
+        wrap_copy.wait_recv()
     normalize(R, 2 * tokens)
     project(1, (Z, R))
     project(2, (Z, R))
@@ -328,6 +347,10 @@
         bias = jnp.where(lane == slot, jnp.where(ok, 0.0, -1e30), bias)
     pair = 2 * HDIM
     first = lax.broadcasted_iota(jnp.int32, (1, pair), 1) < HDIM
+
+    def rolled(j):
+        at = pl.ds(pl.multiple_of(j * pair, pair), pair)
+        return remote(mix_out.at[j], mix.at[:, at], roll_send.at[j], roll_recv.at[j], following, t)
 
     def heads(j, carry):
         at = pl.ds(pl.multiple_of(j * pair, pair), pair)
@@ -349,8 +372,9 @@
             outs.append(att.astype(jnp.bfloat16).astype(jnp.float32))
         mixture = outs[1] + guidance * (outs[0] - outs[1])
         upper = mixture.astype(jnp.bfloat16)
-        mix[0:tokens, at] = upper
-        mix[tokens : 2 * tokens, at] = (mixture - upper.astype(jnp.float32)).astype(jnp.bfloat16)
+        mix_out[j, 0:tokens] = upper
+        mix_out[j, tokens : 2 * tokens] = (mixture - upper.astype(jnp.float32)).astype(jnp.bfloat16)
+        rolled(j).start()
         return carry
 
     lax.fori_loop(0, cols // pair, heads, 0)
@@ -366,22 +390,22 @@
     def hand(j):
         return remote(give.at[j], take.at[j], give_send.at[j], take_recv.at[j], p, o)
 
-    def rolled(j):
-        return remote(stage.at[j], out_ref.at[:, j * OUT_TILE : (j + 1) * OUT_TILE],
-                      roll_send.at[j], roll_recv.at[j], following, t)
-
+    for j in range(cols // pair):
+        rolled(j).wait_recv()
+    coef_copy.wait_recv()
     for j in range(tiles):
         give[j] = partial(o, j)
         hand(j).start()
-    keep = keep_ref[step]
-    noise = noise_ref[step]
+    keep = coefs[1, 0, 0:1, 0:1]
+    noise = coefs[1, 1, 0:1, 0:1]
+    before = low * X + (1 - low) * R
     for j in range(tiles):
+        at = slice(j * OUT_TILE, (j + 1) * OUT_TILE)
         mine = partial(t, j)
         hand(j).wait_recv()
         guided = mine + take[j]
-        current = frames[OWN, t, :, j * OUT_TILE : (j + 1) * OUT_TILE].astype(jnp.float32)
-        stage[j] = (keep * current - noise * guided).astype(stage.dtype)
-        rolled(j).start()
+        current = frames[before, t, :, at].astype(jnp.float32)
+        out_ref[:, at] = (keep * current - noise * guided).astype(out_ref.dtype)
 
     for c in range(CHUNKS):
         own_to(X, c).wait_send()
@@ -410,7 +434,13 @@
             mod_to(d).wait_send()
     for j in range(tiles):
         hand(j).wait_send()
-        rolled(j).wait()
+    for j in range(cols // pair):
+        rolled(j).wait_send()
+    coef_copy.wait_send()
+
+    @pl.when(p == n - 1)
+    def _():
+        wrap_copy.wait_send()
 
 
 def on_device(
@@ -421,6 +451,7 @@
     _, tokens, half = latent.shape
     cols = w_qkv.shape[2]
     tiles = half // OUT_TILE
+    pairs = cols // (2 * HDIM)
     dma = pltpu.SemaphoreType.DMA
     bf16, f32 = jnp.bfloat16, jnp.float32
     smem = pl.BlockSpec(memory_space=pltpu.SMEM)
@@ -443,12 +474,14 @@
             pltpu.VMEM((2 * tokens, cols), bf16),
             pltpu.VMEM((tiles, tokens, OUT_TILE), f32),
             pltpu.VMEM((tiles, tokens, OUT_TILE), f32),
-            pltpu.VMEM((tiles, tokens, OUT_TILE), bf16),
+            pltpu.VMEM((pairs, 2 * tokens, 2 * HDIM), bf16),
+            pltpu.VMEM((2, 2, 8, 128), f32),
             dma, dma((3,)), dma,
             dma((SPAN,)), dma((SPAN,)),
             dma((SPAN, CHUNKS)), dma((SPAN, CHUNKS)),
             dma((2, CHUNKS)), dma((CHUNKS,)), dma((CHUNKS,)), dma((4, CHUNKS)),
-            dma((tiles,)), dma((tiles,)), dma((tiles,)), dma((tiles,)),
+            dma((tiles,)), dma((tiles,)), dma((pairs,)), dma((pairs,)),
+            dma, dma, dma, dma,
         ],
         compiler_params=pltpu.CompilerParams(
             collective_id=0, has_side_effects=True, vmem_limit_bytes=62 * 1024 * 1024

time: 71.1 us -> 68.8 us (0.968)
  the two profiles are of different devices: /device:TPU:0 before, /device:TPU:9 now
where the time goes in v2:
time: 68.8 us; the launch traced here: 68.7 us
  Pallas kernels  64.9 us (94%)
  between operations  1.95 us (3%)
  local copies, waits for them, and re-layouts  1.77 us (3%)
    pallas_call x1, Pallas kernels, on_device(): pl.pallas_call(functools.partial(kernel, n), out_shape=jax.ShapeDtypeStru...  64.9 us
    unnamed x1, local copies, waits for them, and re-layouts  1.77 us

profile of v2, /device:TPU:9, one launch (start us, length us, event | category | flops | bytes accessed | tf_op | source)
XLA Modules:
  0.0 68.7 jit_solution(5601744664335576177)
XLA Ops:
  1.9 64.9 %shard_map.100 = bf16[128,1536]{1,0:T(8,128)(2,1)} custom-call(s32[1]{0:T(128)S(6)} %copy.12.step_ref, s32[1]{0:T(128)S(6)} %copy.13.back_ref, s32[1]{0:T(128)S(6)} %copy.14.ahead_ref, f32[50]{0:T(128)} %keep_ref.1, f32[50]{0:T(128)} %noise_ref.1, f32[50,2,3072]{2,1,0:T(2,128)} %level_ref.1, f32[2,2,3072]{2,1,0:T(2,128)} %text_ref.1, ...), custom_call_target="tpu_custom_call" | custom-call | tf_op jit(solution)/shard_map/pallas_call | solution.py:460
  66.9 1.8 %copy.15 = bf16[1,128,1536]{2,1,0:T(8,128)(2,1)} copy(bf16[1,128,1536]{2,1,0:T(8,128)(2,1)} %bitcast.1) | data formatting | bytes 786432

commit v3 on v2

--- a/solution.py
+++ b/solution.py
@@ -15,6 +15,7 @@
 MESH = pl.DeviceIdType.MESH
 
 CHUNKS = 4
+SPLIT = CHUNKS // 2
 TILE = 256
 OUT_TILE = 512
 ROWS = 16
@@ -48,6 +49,7 @@
     take,
     mix_out,
     coefs,
+    far,
     own_sem,
     wq_sem,
     wo_sem,
@@ -67,6 +69,8 @@
     coef_recv,
     wrap_send,
     wrap_recv,
+    far_send,
+    far_recv,
 ):
     p = lax.axis_index("queue")
     t = lax.axis_index("tp")
@@ -173,7 +177,18 @@
 
     def slot_to_r(slot, c):
         return remote(piece(slot, t, c), piece(R, t, c),
-                      r_send.at[c], ici_recv.at[R - X, c], xp, t)
+                      r_send.at[c], ici_recv.at[R - X, c], xp if c < SPLIT else yp, t)
+
+    def far_piece(c):
+        return far.at[pl.ds((c - SPLIT) * rows_c, rows_c)]
+
+    def x_to_far(c):
+        return remote(piece(X, t, c), far_piece(c),
+                      far_send.at[c - SPLIT], far_recv.at[c - SPLIT], zfrom, t)
+
+    def far_to_r(c):
+        return remote(far_piece(c), piece(R, t, c),
+                      r_send.at[c], ici_recv.at[R - X, c], yp, t)
 
     def mod_to(d):
         return remote(mods.at[REACH], mods.at[REACH - d],
@@ -181,7 +196,7 @@
 
     for c in range(CHUNKS):
         own_to(Y, c).start()
-        own_to(X, c).start()
+        own_to(X, (c + SPLIT) % CHUNKS).start()
         to_partner(OWN, c).start()
     for d in (1, -1, 2, -2):
         @pl.when((p + d >= 0) & (p + d < n))
@@ -202,7 +217,22 @@
 
     def relay_x(c):
         arrived(X, c)
+        if c >= SPLIT:
+            @pl.when(relays_y)
+            def _():
+                slot_to_r(X, c).start()
+
+            @pl.when(relays_z & has_zfrom)
+            def _():
+                x_to_far(c).start()
         to_partner(X, c).start()
+
+    def relay_far(c):
+        @pl.when(relays_z & has_zto)
+        def _():
+            remote(far_piece(c), far_piece(c), far_send.at[c - SPLIT],
+                   far_recv.at[c - SPLIT], xp, t).wait_recv()
+            far_to_r(c).start()
 
     def relay_y(c):
         arrived(Y, c)
@@ -211,9 +241,10 @@
         def _():
             y_to_z(c).start()
 
-        @pl.when(relays_y)
-        def _():
-            slot_to_r(Y, c).start()
+        if c < SPLIT:
+            @pl.when(relays_y)
+            def _():
+                slot_to_r(Y, c).start()
         to_partner(Y, c).start()
 
     def relay_z(c):
@@ -221,9 +252,10 @@
         def _():
             arrived(Z, c)
 
-            @pl.when(relays_z)
-            def _():
-                slot_to_r(Z, c).start()
+            if c < SPLIT:
+                @pl.when(relays_z)
+                def _():
+                    slot_to_r(Z, c).start()
             to_partner(Z, c).start()
 
     def relay_r(c):
@@ -232,7 +264,7 @@
             arrived(R, c)
             to_partner(R, c).start()
 
-    def normalize(slot, base):
+    def normalize(slot, base, start=0, stop=CHUNKS):
         modulation = mods[REACH + offsets[slot]]
         text = text_ref[...]
         shift = [modulation[0:1] + text[b, 0:1] for b in range(2)]
@@ -256,7 +288,7 @@
                     ).astype(nbuf.dtype)
             return carry
 
-        lax.fori_loop(0, tokens // ROWS, body, 0, unroll=2)
+        lax.fori_loop(start * rows_c // ROWS, stop * rows_c // ROWS, body, 0, unroll=4)
 
     def project(kind, slots):
         m = 2 * tokens * len(slots)
@@ -287,49 +319,56 @@
             remote(mods.at[REACH + d], mods.at[REACH + d], mod_send.at[REACH],
                    mod_recv.at[REACH + d], p, o).wait_recv()
 
-    for c in range(CHUNKS):
-        from_partner(OWN, c).wait_recv()
+    def full(slot, chunks, cond=None):
+        def waits():
+            for c in chunks:
+                from_partner(slot, c).wait_recv()
+        if cond is None:
+            waits()
+        else:
+            pl.when(cond)(waits)
+
+    full(OWN, range(CHUNKS))
     normalize(OWN, 0)
+    relay_y(0)
+    relay_x(2)
     w_copies[0].wait()
     project(0, (OWN,))
-    relay_y(0)
-    relay_x(0)
     w_copies[1].wait()
     project(1, (OWN,))
     relay_y(1)
-    relay_x(1)
+    relay_x(3)
     w_copies[2].wait()
     project(2, (OWN,))
+    relay_far(2)
+    relay_z(0)
     for d in (1, -1, 2, -2):
         mod_arrives(d)
-    for c in range(2, CHUNKS):
-        relay_y(c)
-        relay_z(c - 2)
-        relay_x(c)
-    for c in range(CHUNKS):
-        from_partner(X, c).wait_recv()
-    normalize(X, 0)
-    for c in range(CHUNKS):
-        from_partner(Y, c).wait_recv()
+    full(X, (2, 3))
+    normalize(X, 0, 2, 4)
+    relay_y(2)
+    relay_x(0)
+    relay_far(3)
+    relay_z(1)
+    full(Y, (0, 1))
+    normalize(Y, 2 * tokens, 0, 2)
     relay_r(0)
-    normalize(Y, 2 * tokens)
+    relay_r(2)
+    relay_y(3)
+    relay_x(1)
+    full(X, (0, 1))
+    normalize(X, 0, 0, 2)
     relay_z(2)
+    full(Y, (2, 3))
+    normalize(Y, 2 * tokens, 2, 4)
+    relay_z(3)
     project(1, (X, Y))
-    relay_z(3)
     relay_r(1)
+    relay_r(3)
     project(2, (X, Y))
-    relay_r(2)
-
-    def slot_full(slot, cond):
-        @pl.when(cond)
-        def _():
-            for c in range(CHUNKS):
-                from_partner(slot, c).wait_recv()
-
-    slot_full(Z, has_zfrom)
+    full(Z, range(CHUNKS), has_zfrom)
     normalize(Z, 0)
-    relay_r(3)
-    slot_full(R, has_r)
+    full(R, range(CHUNKS), has_r)
 
     @pl.when(p == 0)
     def _():
@@ -421,9 +460,14 @@
         def _(c=c):
             to_partner(Z, c).wait_send()
 
-        @pl.when(relays_y | has_zfrom)
+        @pl.when(relays_y | (has_zfrom if c < SPLIT else has_zto))
         def _(c=c):
             slot_to_r(Y, c).wait_send()
+
+        if c >= SPLIT:
+            @pl.when(relays_z & has_zfrom)
+            def _(c=c):
+                x_to_far(c).wait_send()
 
         @pl.when(has_r)
         def _(c=c):
@@ -476,12 +520,13 @@
             pltpu.VMEM((tiles, tokens, OUT_TILE), f32),
             pltpu.VMEM((pairs, 2 * tokens, 2 * HDIM), bf16),
             pltpu.VMEM((2, 2, 8, 128), f32),
+            pltpu.VMEM((tokens // 2, half), bf16),
             dma, dma((3,)), dma,
             dma((SPAN,)), dma((SPAN,)),
             dma((SPAN, CHUNKS)), dma((SPAN, CHUNKS)),
             dma((2, CHUNKS)), dma((CHUNKS,)), dma((CHUNKS,)), dma((4, CHUNKS)),
             dma((tiles,)), dma((tiles,)), dma((pairs,)), dma((pairs,)),
-            dma, dma, dma, dma,
+            dma, dma, dma, dma, dma((CHUNKS - SPLIT,)), dma((CHUNKS - SPLIT,)),
         ],
         compiler_params=pltpu.CompilerParams(
             collective_id=0, has_side_effects=True, vmem_limit_bytes=62 * 1024 * 1024

time: 68.8 us -> 65.4 us (0.951)
  the two profiles are of different devices: /device:TPU:9 before, /device:TPU:11 now
where the time goes in v3:
time: 65.4 us; the launch traced here: 65.2 us
  Pallas kernels  61.5 us (94%)
  between operations  1.95 us (3%)
  local copies, waits for them, and re-layouts  1.77 us (3%)
    pallas_call x1, Pallas kernels, on_device(): pl.pallas_call(functools.partial(kernel, n), out_shape=jax.ShapeDtypeStru...  61.5 us
    unnamed x1, local copies, waits for them, and re-layouts  1.77 us

profile of v3, /device:TPU:11, one launch (start us, length us, event | category | flops | bytes accessed | tf_op | source)
XLA Modules:
  0.0 65.2 jit_solution(4404574883824731586)
XLA Ops:
  1.9 61.5 %shard_map.100 = bf16[128,1536]{1,0:T(8,128)(2,1)} custom-call(s32[1]{0:T(128)S(6)} %copy.12.step_ref, s32[1]{0:T(128)S(6)} %copy.13.back_ref, s32[1]{0:T(128)S(6)} %copy.14.ahead_ref, f32[50]{0:T(128)} %keep_ref.1, f32[50]{0:T(128)} %noise_ref.1, f32[50,2,3072]{2,1,0:T(2,128)} %level_ref.1, f32[2,2,3072]{2,1,0:T(2,128)} %text_ref.1, ...), custom_call_target="tpu_custom_call" | custom-call | tf_op jit(solution)/shard_map/pallas_call | solution.py:504
  63.4 1.8 %copy.15 = bf16[1,128,1536]{2,1,0:T(8,128)(2,1)} copy(bf16[1,128,1536]{2,1,0:T(8,128)(2,1)} %bitcast.1) | data formatting | bytes 786432
